TPU v7x, 128 devices: a whole 4x4x4 slice. The times are simulated.
128 devices in a mesh: replica: 8 (over x, y_hi), shard: 16 (over z, y_lo, core).
Axes of the slice: x: 4, y: 4 (y_hi: 2, y_lo: 2; y = y_hi * 2 + y_lo), z: 4, core: 2. Of those that a mesh axis runs over, the one named last changes fastest.
Arguments:
- tokens: bfloat16 [65536, 1920], P(('replica', 'shard')), may hold values from -36 to 36
- timesteps: int32 [256], P(('replica', 'shard')), may hold values from 0 to 63
- table: float32 [64, 2, 1920], replicated, may hold values from -3 to 3
- weight_values: bfloat16 [4864, 1920], P('shard'), may hold values from -0.125 to 0.125
- weight_scales: bfloat16 [4864, 15], P('shard'), may hold values from 0.29882812 to 3
- cotangent: bfloat16 [65536, 4864], P(('replica', 'shard')), may hold values from -24 to 24
Outputs:
- hidden: bfloat16 [65536, 4864], P(('replica', 'shard'))
- grad_weight: float32 [4864, 1920], P('shard')
- grad_tokens: bfloat16 [65536, 1920], P(('replica', 'shard'))
All inputs are finite; a program needn't handle non-finite values.
Results may differ from a plain program's by a relative error of at most 0.02.
Values may be sent and summed in bfloat16 or wider, within the bound.
A program may use at most 256 MiB of HBM per device.

v0:
```python
import jax
import jax.numpy as jnp
from jax import lax
from jax.sharding import PartitionSpec as P

root_two_over_pi = 0.7978845608028654
cubic_coef = 0.044715
epsilon = 1e-06


def gelu_slope(preact):
    inner_term = root_two_over_pi * (preact + cubic_coef * preact * preact * preact)
    tangent = jnp.tanh(inner_term)
    gelu_value = 0.5 * preact * (1.0 + tangent)
    derivative = 0.5 * (1.0 + tangent) + 0.5 * preact * (
        1.0 - tangent * tangent
    ) * root_two_over_pi * (1.0 + 3.0 * cubic_coef * preact * preact)
    return (gelu_value, derivative)


def dequantize(weight_values, weight_scales):
    row_count, features = weight_values.shape
    blocks = weight_scales.shape[1]
    expanded = (
        weight_values.astype(jnp.float32).reshape(row_count, blocks, features // blocks)
        * weight_scales.astype(jnp.float32)[:, :, None]
    )
    return expanded.reshape(row_count, features).astype(jnp.bfloat16)


def modulate(tokens, timesteps, table):
    samples = timesteps.shape[0]
    step_count = table.shape[0]
    features = tokens.shape[1]
    onehot = (timesteps[:, None] == jnp.arange(step_count, dtype=jnp.int32)[None, :]).astype(
        jnp.float32
    )
    picked = jnp.dot(
        onehot, table.reshape(step_count, 2 * features), precision=lax.Precision.HIGHEST
    )
    picked = picked.reshape(samples, 2, features)
    grouped = tokens.astype(jnp.float32).reshape(samples, -1, features)
    centre = grouped - jnp.mean(grouped, axis=2, keepdims=True)
    inverse = lax.rsqrt(jnp.mean(centre * centre, axis=2, keepdims=True) + epsilon)
    normed = centre * inverse
    factor = 1.0 + picked[:, 1][:, None, :]
    moved = (normed * factor + picked[:, 0][:, None, :]).reshape(-1, features).astype(jnp.bfloat16)
    return (moved, normed, inverse, factor)


def normalize_back(grad_moved, normed, inverse, factor):
    samples = normed.shape[0]
    features = normed.shape[2]
    scaled_grad = grad_moved.reshape(samples, -1, features) * factor
    mean_grad = jnp.mean(scaled_grad, axis=2, keepdims=True)
    mean_prod = jnp.mean(scaled_grad * normed, axis=2, keepdims=True)
    result = inverse * (scaled_grad - mean_grad - normed * mean_prod)
    return result.reshape(-1, features).astype(jnp.bfloat16)


def per_device(tokens, timesteps, table, weight_values, weight_scales, cotangent):
    moved, normed, inverse, factor = modulate(tokens, timesteps, table)
    upstream = cotangent.astype(jnp.float32)
    weight = lax.all_gather(dequantize(weight_values, weight_scales), "shard", axis=0, tiled=True)
    preact = jnp.einsum("td,fd->tf", moved, weight, preferred_element_type=jnp.float32)
    gelu_value, derivative = gelu_slope(preact)
    hidden = gelu_value.astype(jnp.bfloat16)
    grad_pre = (upstream * derivative).astype(jnp.bfloat16)
    grad_moved = jnp.dot(grad_pre, weight, preferred_element_type=jnp.float32)
    product = lax.dot_general(
        grad_pre, moved, (((0,), (0,)), ((), ())), preferred_element_type=jnp.float32
    )
    rounded = lax.optimization_barrier(product.astype(jnp.bfloat16))
    group_part = lax.psum_scatter(
        rounded.astype(jnp.float32).astype(jnp.bfloat16), "shard", scatter_dimension=0, tiled=True
    )
    grad_weight = lax.psum(group_part, "replica").astype(jnp.float32)
    grad_tokens = normalize_back(grad_moved, normed, inverse, factor)
    return (hidden, grad_weight, grad_tokens)


def solution(mesh):
    placed = (
        P(("replica", "shard"), None),
        P(("replica", "shard")),
        P(),
        P("shard", None),
        P("shard", None),
        P(("replica", "shard"), None),
    )
    return jax.shard_map(
        per_device,
        mesh=mesh,
        in_specs=placed,
        out_specs=(P(("replica", "shard"), None), P("shard", None), P(("replica", "shard"), None)),
        check_vma=False,
    )
```

profile of v0, /device:TPU:0, one launch (start us, length us, event | category | flops | bytes accessed | tf_op | source)
XLA Modules:
  0.0 461.4 jit_solution(8686879250005387591)
XLA Ops:
  7.2 0.0 copy-start
  7.2 0.0 copy-start.1
  7.2 0.0 copy-start.2
  7.2 0.0 all-gather.2.cloned.1.call-start
  7.2 1.0 copy.11
  8.2 0.7 mul.124
  8.9 3.1 fusion.18
  12.0 0.0 all-gather.2.cloned.1.call-update
  12.0 0.0 reduce-scatter.2.cloned.1.call-start
  12.1 0.0 copy-done
  12.1 0.3 convert_reduce_fusion
  12.4 0.7 fusion.15
  13.1 0.0 copy-done.1
  13.1 0.0 copy-done.2
  13.1 0.4 fusion.19
  13.6 2.5 fusion.17
  16.1 99.2 %all-gather.2.cloned.1.call-done = bf16[4864,1920]{1,0:T(8,128)(2,1)} async-done(((bf16[304,1920]{1,0:T(8,128)(2,1)}), bf16[4864,1920]{1,0:T(8,128)(2,1)}) %all-gather.2.cloned.1.call-update) | async-done | bytes 18677776 | tf_op jit(solution)/shard_map/all_gather | solution.py:64
  115.3 18.7 %multiply_convert_fusion = (bf16[512,4864]{1,0:T(8,128)(2,1)}, f32[512,4864]{1,0:T(8,128)}) fusion(bf16[512,1920]{1,0:T(8,128)(2,1)} %fusion.17, bf16[4864,1920]{1,0:T(8,128)(2,1)} %all-gather.2.cloned.1.call-done), kind=kOutput, calls=%fused_computation.10 | convolution fusion | flops 9585426432 | bytes 35586048 | tf_op jit(solution)/shard_map/td,fd->tf/dot_general | solution.py:65
  134.0 23.2 %convolution_convert_fusion = bf16[4864,1920]{1,0:T(8,128)(2,1)} fusion(bf16[512,1920]{1,0:T(8,128)(2,1)} %fusion.17, f32[512,4864]{1,0:T(8,128)} %get-tuple-element.8, bf16[512,4864]{1,0:T(8,128)(2,1)} %param.11), kind=kOutput, calls=%fused_computation | convolution fusion | flops 9622159360 | bytes 35586048 | tf_op jit(solution)/shard_map/dot_general | solution.py:70
  157.2 0.0 reduce-scatter.2.cloned.1.call-update
  157.2 0.0 all-reduce.2.cloned.1.call-start
  157.3 203.4 %reduce-scatter.2.cloned.1.call-done = bf16[304,1920]{1,0:T(8,128)(2,1)} async-done(((bf16[4864,1920]{1,0:T(8,128)(2,1)}), bf16[304,1920]{1,0:T(8,128)(2,1)}) %reduce-scatter.2.cloned.1.call-update) | async-done | bytes 1167376 | tf_op jit(solution)/shard_map/reduce_scatter | solution.py:74
  360.7 0.0 all-reduce.2.cloned.1.call-update
  360.7 23.9 %fusion.29 = (f32[512]{0:T(512)S(1)}, f32[512]{0:T(512)S(1)}, f32[512,1920]{1,0:T(8,128)S(1)}) fusion(f32[512]{0:T(512)S(1)} %add_rsqrt_fusion, f32[512]{0:T(512)S(1)} %broadcast_multiply_fusion.2, bf16[512,1920]{1,0:T(8,128)(2,1)S(1)} %copy-done, f32[2,1920]{1,0:T(2,128)S(1)} %get-tuple-element.5, bf16[4864,1920]{1,0:T(8,128)(2,1)} %all-gather.2.cloned.1.call-done, ...), kind=kOutput, calls=%fused_computation.42 | convolution fusion | flops 9619701760 | bytes 39541760 | tf_op jit(solution)/shard_map/dot_general | solution.py:69
  384.6 2.4 fusion.14
  387.0 65.1 %all-reduce.2.cloned.1.call-done = bf16[304,1920]{1,0:T(8,128)(2,1)} async-done(((bf16[304,1920]{1,0:T(8,128)(2,1)}), bf16[304,1920]{1,0:T(8,128)(2,1)}) %all-reduce.2.cloned.1.call-update) | async-done | bytes 1167376 | tf_op jit(solution)/shard_map/psum | solution.py:77
  452.1 2.8 convert_element_type.45
  (4 shorter events, 0.0 us)
Async XLA Ops:
  7.2 4.9 %copy-start = (bf16[512,1920]{1,0:T(8,128)(2,1)S(1)}, bf16[512,1920]{1,0:T(8,128)(2,1)}, u32[]{:S(2)}) copy-start(bf16[512,1920]{1,0:T(8,128)(2,1)} %param.6) | copy-start | bytes 5898244
  7.2 5.9 %copy-start.1 = (f32[64,2,1920]{2,1,0:T(2,128)S(1)}, f32[64,2,1920]{2,1,0:T(2,128)}, u32[]{:S(2)}) copy-start(f32[64,2,1920]{2,1,0:T(2,128)} %param.8) | copy-start | bytes 2949124
  7.2 5.9 %copy-start.2 = (s32[2]{0:T(128)S(1)}, s32[2]{0:T(128)}, u32[]{:S(2)}) copy-start(s32[2]{0:T(128)} %param.7) | copy-start | bytes 28
  7.2 108.1 %all-gather.2.cloned.1.call-start = ((), (), s32[]{:S(2)}) async-start(), calls=%async_computation.1 | async-start | bytes 19845120 | tf_op jit(solution)/shard_map/all_gather | solution.py:64
  12.0 348.6 %reduce-scatter.2.cloned.1.call-start = ((), (), s32[]{:S(2)}) async-start(), calls=%async_computation.2 | async-start | bytes 19845120 | tf_op jit(solution)/shard_map/reduce_scatter | solution.py:74
  157.2 294.8 %all-reduce.2.cloned.1.call-start = ((), (), s32[]{:S(2)}) async-start(), calls=%async_computation.3 | async-start | bytes 2334720 | tf_op jit(solution)/shard_map/psum | solution.py:77
Sparse Core Ops, SparseCore 0:
  12.2 103.0 all-gather.1
  157.4 203.2 reduce-scatter.1
  363.4 88.6 all-reduce.1
where the time goes:
time: 462 us; the launch traced here: 461 us
  waiting for transfers between devices  368 us (80%)
  matrix products  66.3 us (14%)
  between operations  13.8 us (3%)
  other arithmetic  11.8 us (3%)
    reduce_scatter x1, waiting for transfers between devices, per_device(): lax.psum_scatter(rounded.astype(jnp.float32).astype(jnp.bfloat16), 'shard...  203 us
    all_gather x1, waiting for transfers between devices, per_device(): lax.all_gather(dequantize(weight_values, weight_scales), 'shard', axis=0,...  99.2 us
    psum x1, waiting for transfers between devices, per_device(): grad_weight = lax.psum(group_part, 'replica').astype(jnp.float32)  65.1 us
    dot_general x1, matrix products, per_device(): grad_moved = jnp.dot(grad_pre, weight, preferred_element_type=jnp.float32)  23.9 us
    dot_general x1, matrix products, per_device(): lax.dot_general(grad_pre, moved, (((0,), (0,)), ((), ())), preferred_elem...  23.2 us
    dot_general x1, matrix products, per_device(): jnp.einsum('td,fd->tf', moved, weight, preferred_element_type=jnp.float32)  18.7 us
  transfers between devices with their start and end apart: 3, of which 3 were waited for; matrix products, arithmetic and copies ran while one was open for 7% of the time, Pallas kernels for 0%

commit v1 on v0

--- a/solution.py
+++ b/solution.py
@@ -6,6 +6,13 @@
 root_two_over_pi = 0.7978845608028654
 cubic_coef = 0.044715
 epsilon = 1e-06
+
+
+def exchange_gather(shard, name, along):
+    size = lax.axis_size(name)
+    pieces = jnp.stack([shard for _ in range(size)])
+    pieces = lax.all_to_all(pieces, name, split_axis=0, concat_axis=0)
+    return jnp.concatenate(pieces, axis=along)
 
 
 def gelu_slope(preact):
@@ -61,7 +68,7 @@
 def per_device(tokens, timesteps, table, weight_values, weight_scales, cotangent):
     moved, normed, inverse, factor = modulate(tokens, timesteps, table)
     upstream = cotangent.astype(jnp.float32)
-    weight = lax.all_gather(dequantize(weight_values, weight_scales), "shard", axis=0, tiled=True)
+    weight = exchange_gather(dequantize(weight_values, weight_scales), "shard", 0)
     preact = jnp.einsum("td,fd->tf", moved, weight, preferred_element_type=jnp.float32)
     gelu_value, derivative = gelu_slope(preact)
     hidden = gelu_value.astype(jnp.bfloat16)

time: 462 us -> 572 us (1.24)
  waiting for transfers between devices: 368 us -> 476 us
  matrix products: 66.3 us -> 56 us
  starting transfers between devices: 0.12 us -> 6.77 us
  local copies, waits for them, and re-layouts: 1.69 us -> 8.31 us
    all_to_all x0 -> x1, waiting for transfers between devices: none -> 201 us  [exchange_gather(): pieces = lax.all_to_all(pieces, name, split_axis=0, concat_axis=0)]
    all_gather x1 -> x0, waiting for transfers between devices: 99.2 us -> none  [per_device(): lax.all_gather(dequantize(weight_values, weight_scales), 'shard', axis=0,...]
    dot_general x1, matrix products: 23.9 us -> 16.2 us  [per_device(): grad_moved = jnp.dot(grad_pre, weight, preferred_element_type=jnp.float32)]
    psum x1, waiting for transfers between devices: 65.1 us -> 72.6 us  [per_device(): grad_weight = lax.psum(group_part, 'replica').astype(jnp.float32)]
    all_to_all x0 -> x1, starting transfers between devices: none -> 6.69 us  [exchange_gather(): pieces = lax.all_to_all(pieces, name, split_axis=0, concat_axis=0)]
    another operation x0 -> x1, local copies, waits for them, and re-layouts: none -> 6.62 us  [exchange_gather(): pieces = jnp.stack([shard for _ in range(size)])]
    dot_general x1, matrix products: 23.2 us -> 16.6 us  [per_device(): lax.dot_general(grad_pre, moved, (((0,), (0,)), ((), ())), preferred_elem...]
  transfers between devices with their start and end apart: 3 -> 3, of which waited for: 3 -> 3; matrix products, arithmetic and copies ran while one was open for 7% -> 4% of each run, Pallas kernels for 0% -> 0%
where the time goes in v1:
time: 572 us
  waiting for transfers between devices  476 us (83%)
  matrix products  56 us (10%)
  between operations  14.1 us (2%)
  other arithmetic  10.8 us (2%)
  local copies, waits for them, and re-layouts  8.31 us (1%)
  starting transfers between devices  6.77 us (1%)
    reduce_scatter x1, waiting for transfers between devices, per_device(): lax.psum_scatter(rounded.astype(jnp.float32).astype(jnp.bfloat16), 'shard...  202 us
    all_to_all x1, waiting for transfers between devices, exchange_gather(): pieces = lax.all_to_all(pieces, name, split_axis=0, concat_axis=0)  201 us
    psum x1, waiting for transfers between devices, per_device(): grad_weight = lax.psum(group_part, 'replica').astype(jnp.float32)  72.6 us
    dot_general x1, matrix products, per_device(): jnp.einsum('td,fd->tf', moved, weight, preferred_element_type=jnp.float32)  22.7 us
    dot_general x1, matrix products, per_device(): lax.dot_general(grad_pre, moved, (((0,), (0,)), ((), ())), preferred_elem...  16.6 us
    dot_general x1, matrix products, per_device(): grad_moved = jnp.dot(grad_pre, weight, preferred_element_type=jnp.float32)  16.2 us
  transfers between devices with their start and end apart: 3, of which 3 were waited for; matrix products, arithmetic and copies ran while one was open for 4% of the time, Pallas kernels for 0%

profile of v1, /device:TPU:0, one launch (start us, length us, event | category | flops | bytes accessed | tf_op | source)
XLA Modules:
  0.0 572.0 jit_solution(15016844571071779987)
XLA Ops:
  7.2 0.8 copy.11
  8.0 0.7 mul.120
  8.7 2.1 fusion.8
  10.8 6.6 %stack.2 = bf16[16,304,1920]{2,1,0:T(8,128)(2,1)} broadcast(bf16[304,1920]{1,0:T(8,128)(2,1)S(1)} %fusion.8), dimensions={1,2} | broadcast | bytes 19845120 | tf_op jit(solution)/shard_map/stack | solution.py:13
  17.4 0.0 copy-start
  17.4 6.7 %all-to-all-start = ((bf16[16,304,1920]{2,1,0:T(8,128)(2,1)}), bf16[16,304,1920]{2,1,0:T(8,128)(2,1)}, u32[]{:S(2)}, u32[]{:S(2)}) async-start(bf16[16,304,1920]{2,1,0:T(8,128)(2,1)} %stack.2), calls=%async_computation | async-start | bytes 37355520 | tf_op jit(solution)/shard_map/all_to_all | solution.py:14
  24.1 0.0 copy-start.1
  24.1 0.0 copy-start.2
  24.1 0.0 reduce-scatter.2.cloned.1.call-start
  24.2 0.0 copy-done
  24.2 0.3 convert_reduce_fusion
  24.5 0.7 multiply_reduce_fusion.1
  25.2 0.1 copy-done.1
  25.3 0.0 copy-done.2
  25.3 0.4 fusion.9
  25.8 2.5 fusion.7
  28.2 201.5 %all-to-all-done = bf16[16,304,1920]{2,1,0:T(8,128)(2,1)} async-done(((bf16[16,304,1920]{2,1,0:T(8,128)(2,1)}), bf16[16,304,1920]{2,1,0:T(8,128)(2,1)}, u32[]{:S(2)}, u32[]{:S(2)}) %all-to-all-start) | async-done | bytes 18677792 | tf_op jit(solution)/shard_map/all_to_all | solution.py:14
  229.7 22.7 %fusion.6 = (bf16[512,4864]{1,0:T(8,128)(2,1)}, bf16[512,4864]{1,0:T(8,128)(2,1)}) fusion(bf16[512,4864]{1,0:T(8,128)(2,1)} %param.11, bf16[512,1920]{1,0:T(8,128)(2,1)} %fusion.7, bf16[4864,1920]{1,0:T(8,128)(2,1)} %bitcast.6), kind=kOutput, calls=%fused_computation.9 | convolution fusion | flops 9617801216 | bytes 35586048 | tf_op jit(solution)/shard_map/td,fd->tf/dot_general | solution.py:72
  252.4 16.6 %convolution_convert_fusion = bf16[4864,1920]{1,0:T(8,128)(2,1)} fusion(bf16[512,4864]{1,0:T(8,128)(2,1)} %get-tuple-element.5, bf16[512,1920]{1,0:T(8,128)(2,1)} %fusion.7), kind=kOutput, calls=%fused_computation | convolution fusion | flops 9572352000 | bytes 25624576 | tf_op jit(solution)/shard_map/dot_general | solution.py:77
  269.1 0.0 reduce-scatter.2.cloned.1.call-update
  269.1 0.0 all-reduce.2.cloned.1.call-start
  269.2 202.0 %reduce-scatter.2.cloned.1.call-done = bf16[304,1920]{1,0:T(8,128)(2,1)} async-done(((bf16[4864,1920]{1,0:T(8,128)(2,1)}), bf16[304,1920]{1,0:T(8,128)(2,1)}) %reduce-scatter.2.cloned.1.call-update) | async-done | bytes 1167376 | tf_op jit(solution)/shard_map/reduce_scatter | solution.py:81
  471.1 0.0 all-reduce.2.cloned.1.call-update
  471.2 16.2 %fusion.17 = (f32[2,256]{1,0:T(2,128)S(1)}, f32[2,256]{1,0:T(2,128)S(1)}, f32[2,256,1920]{2,1,0:T(8,128)S(1)}) fusion(f32[2,256]{1,0:T(2,128)S(1)} %rsqrt.13, f32[2,256]{1,0:T(2,128)S(1)} %div.17, f32[2,1920]{1,0:T(2,128)S(1)} %get-tuple-element.7, bf16[2,256,4864]{2,1,0:T(8,128)(2,1)} %bitcast.49, bf16[4864,1920,1]{1,0,2:T(8,128)(2,1)} %bitcast.8, ...), kind=kOutput, calls=%fused_computation.36 | convolution fusion | flops 9569894400 | bytes 29580288 | tf_op jit(solution)/shard_map/dot_general | solution.py:76
  487.4 2.4 multiply_convert_fusion.1
  489.8 72.6 %all-reduce.2.cloned.1.call-done = bf16[304,1920]{1,0:T(8,128)(2,1)} async-done(((bf16[304,1920]{1,0:T(8,128)(2,1)}), bf16[304,1920]{1,0:T(8,128)(2,1)}) %all-reduce.2.cloned.1.call-update) | async-done | bytes 1167376 | tf_op jit(solution)/shard_map/psum | solution.py:84
  562.3 2.8 convert_element_type.48
  (6 shorter events, 0.1 us)
Async XLA Ops:
  17.4 6.8 %copy-start = (bf16[512,1920]{1,0:T(8,128)(2,1)S(1)}, bf16[512,1920]{1,0:T(8,128)(2,1)}, u32[]{:S(2)}) copy-start(bf16[512,1920]{1,0:T(8,128)(2,1)} %param.6) | copy-start | bytes 5898244
  17.4 212.3 %all-to-all-start = ((bf16[16,304,1920]{2,1,0:T(8,128)(2,1)}), bf16[16,304,1920]{2,1,0:T(8,128)(2,1)}, u32[]{:S(2)}, u32[]{:S(2)}) async-start(bf16[16,304,1920]{2,1,0:T(8,128)(2,1)} %stack.2), calls=%async_computation | async-start | bytes 37355520 | tf_op jit(solution)/shard_map/all_to_all | solution.py:14
  24.1 1.2 copy-start.1
  24.1 1.2 copy-start.2
  24.1 447.0 %reduce-scatter.2.cloned.1.call-start = ((), (), s32[]{:S(2)}) async-start(), calls=%async_computation.2 | async-start | bytes 19845120 | tf_op jit(solution)/shard_map/reduce_scatter | solution.py:81
  269.1 293.2 %all-reduce.2.cloned.1.call-start = ((), (), s32[]{:S(2)}) async-start(), calls=%async_computation.3 | async-start | bytes 2334720 | tf_op jit(solution)/shard_map/psum | solution.py:84
Sparse Core Ops, SparseCore 0:
  269.2 201.8 reduce-scatter.1
  473.8 88.4 all-reduce.1
